TPU v7x, 512 devices: a whole 4x4x16 slice. The times are simulated.
512 devices in a mesh: expert: 128 (over y, z, core), dp: 4 (over x).
Axes of the slice: x: 4, y: 4, z: 16, core: 2. Of those that a mesh axis runs over, the one named last changes fastest.
Arguments:
- tokens: bfloat16 [12288, 2048], P(('expert', 'dp')), may hold values from -6 to 6
- route_ids: int32 [12288, 8], P(('expert', 'dp')), may hold values from 0 to 127, all different within a row; in each aligned block of 24 rows (0 to 23, 24 to 47, ...) at most 2 rows name the same one
- gates: float32 [12288, 8], P(('expert', 'dp')), may hold values from 0.05 to 0.5
- cotangent: bfloat16 [12288, 2048], P(('expert', 'dp')), may hold values from -1.5 to 1.5
- w_gate_up: bfloat16 [128, 2048, 768], P('expert', 'dp'), may hold values from -0.125 to 0.125
- w_down: bfloat16 [128, 2048, 384], P('expert', 'dp'), may hold values from -0.3125 to 0.3125
Outputs:
- mixed: bfloat16 [12288, 2048], P(('expert', 'dp'))
- grad_tokens: bfloat16 [12288, 2048], P(('expert', 'dp'))
- grad_gates: float32 [12288, 8], P(('expert', 'dp'))
- grad_gate_up: bfloat16 [128, 2048, 768], P('expert', 'dp')
- grad_down: bfloat16 [128, 2048, 384], P('expert', 'dp')
Inputs may be any that keep to these rules, and one draw needn't show every extreme that they name: `route_ids`: each row names 8 different experts. Among the 24 rows of one device no expert is named by more than 2 rows, and in every draw some device's rows name some expert exactly 2 times.
All inputs are finite; a program needn't handle non-finite values.
Results may differ from a plain program's by a relative error of at most 0.0064.
Values may be sent and summed in bfloat16 or wider, within the bound.
A program may use at most 64 MiB of HBM per device.

v0:
```python
import jax
import jax.numpy as jnp
from jax import lax
from jax.experimental import pallas as pl
from jax.experimental.pallas import tpu as pltpu
from jax.sharding import PartitionSpec as P

NX, NY, NZ, NC = 4, 4, 16, 2
GROUP = NY * NC
HALF = NZ // 2
BATCHES = NZ // 4
PAIR = 2
TOKS = 24
TOP = 8
D = 2048
FFW = 384
LANES = 128
TILE = 512
WIDE = 2 * D + LANES
SHARD = D // NX
SLOTS = GROUP * 4 * PAIR
ROWS = BATCHES * SLOTS
N_SEM = 192
F32 = jnp.float32
BF16 = jnp.bfloat16


def positions():
    order = []
    for b in range(BATCHES):
        s = 2 * b + 1
        order += [s, NZ - s, s + 1, NZ - s - 1 if s + 1 < HALF else 0]
    return {d: i for i, d in enumerate(order)}


POS = positions()


def dot(a, b, contract):
    return lax.dot_general(a, b, ((contract[:1], contract[1:]), ((), ())), preferred_element_type=F32)


def columns(i):
    return pl.ds(pl.multiple_of(i * TILE, TILE), TILE)


def three_parts(v):
    high = v.astype(BF16).astype(F32)
    rest = v - high
    middle = rest.astype(BF16).astype(F32)
    return high, middle, rest - middle


def lane_block(v, shape):
    high, middle, low = three_parts(v)
    lane = lax.broadcasted_iota(jnp.int32, shape, len(shape) - 1)
    return jnp.where(
        lane == 0, high, jnp.where(lane == 1, middle, jnp.where(lane == 2, low, 0.0))
    ).astype(BF16)


def kernel(
    tok, cot, meta, wg, wd,
    mixed, gtok, gg, ggu, gd,
    gx, gc, mb, comb, pb, sel, rows, wgf, wdf, pre, ub, hs, pair, ob, cb,
    part, ggp, dm, um, dd, ud, dg, ug, gp_gu, gp_d, x2_gu, x2_d, x1_gu, x1_d,
    send_sem, recv_sem, local_sem,
):
    e = lax.axis_index("expert")
    x = lax.axis_index("dp")
    plane = NZ * NC
    y = e // plane
    z = (e // NC) % NZ
    c = e % NC
    me = y * NC + c
    up = y * plane + ((z + 1) % NZ) * NC + c
    down = y * plane + ((z + NZ - 1) % NZ) * NC + c
    right = (x + 1) % NX
    left = (x + NX - 1) % NX

    def member(m):
        return (m // NC) * plane + z * NC + m % NC

    barrier = pltpu.get_barrier_semaphore()
    peers = [("expert", up), ("expert", down), ("dp", right), ("dp", left)]
    peers += [("expert", member((me + o) % GROUP)) for o in range(1, GROUP)]
    for axis, target in peers:
        pl.semaphore_signal(
            barrier, inc=1, device_id={axis: target}, device_id_type=pl.DeviceIdType.MESH
        )
    pl.semaphore_wait(barrier, len(peers))

    started = []

    def send(src, dst, axis, target):
        i = len(started)
        copy = pltpu.make_async_remote_copy(
            src_ref=src,
            dst_ref=dst,
            send_sem=send_sem.at[i],
            recv_sem=recv_sem.at[i],
            device_id={axis: target},
            device_id_type=pl.DeviceIdType.MESH,
        )
        copy.start()
        started.append(copy)
        return copy

    halves = [pl.ds(h * (SHARD // 2), SHARD // 2) for h in range(2)]
    ring = {}

    def ring_send(s):
        for name, own, buf in (("x", tok, gx), ("c", cot, gc), ("m", meta, mb)):
            if s <= HALF and not (name == "c" and s == HALF):
                src = own
                if s > 1:
                    ring[name, 1, s - 1].wait_recv()
                    src = buf.at[POS[s - 1]]
                ring[name, 1, s] = send(src, buf.at[POS[s]], "expert", up)
            if s < HALF or (name == "c" and s == HALF):
                src = own
                if s > 1:
                    ring[name, -1, s - 1].wait_recv()
                    src = buf.at[POS[NZ - s + 1]]
                ring[name, -1, s] = send(src, buf.at[POS[NZ - s]], "expert", down)

    ring_send(1)

    weights = ((wg, wgf), (wd, wdf))
    to_right, to_left = {}, {}
    for h in range(2):
        for i, (w, full) in enumerate(weights):
            to_right[i, h] = send(w.at[0, halves[h]], full.at[x, halves[h]], "dp", right)
            g = 1 - h
            to_left[i, g] = send(w.at[0, halves[g]], full.at[x, halves[g]], "dp", left)
    keep = [
        pltpu.make_async_copy(w.at[0], full.at[x], local_sem.at[i])
        for i, (w, full) in enumerate(weights)
    ]
    for copy in keep:
        copy.start()
    on_right, on_left = {}, {}

    def pass_weights():
        for i, (w, full) in enumerate(weights):
            to_right[i, 0].wait_recv()
            piece = full.at[left, halves[0]]
            on_right[i] = send(piece, piece, "dp", right)
            to_left[i, 1].wait_recv()
            piece = full.at[right, halves[1]]
            on_left[i] = send(piece, piece, "dp", left)

    gx[POS[0]] = tok[...]
    gc[POS[0]] = cot[...]
    mb[POS[0]] = meta[...]

    lane = lax.broadcasted_iota(jnp.int32, (LANES, LANES), 1)
    line = lax.broadcasted_iota(jnp.int32, (LANES, LANES), 0)

    def source_of(index):
        total = jnp.zeros(index.shape, jnp.int32)
        for j in range(1, 5):
            total = total + jnp.where(index >= j * TOKS, 1, 0)
        return total

    earlier = jnp.where((line < lane) & (source_of(line) == source_of(lane)), 1.0, 0.0).astype(F32)
    member_line = lax.broadcasted_iota(jnp.int32, (GROUP, LANES), 0)
    expert_line = ((member_line >> 1) * plane + z * NC + (member_line & 1) + 1).astype(F32)
    cube = (GROUP, 4 * PAIR, LANES)
    cube_row = lax.broadcasted_iota(jnp.int32, cube, 1)
    cube_source = source_of(lax.broadcasted_iota(jnp.int32, cube, 2))

    def choose(b):
        tiles = mb[4 * b]
        for j in range(1, 4):
            tiles = tiles + pltpu.roll(mb[4 * b + j], TOKS * j, 1)
        comb[b] = tiles
        hits = jnp.zeros((GROUP, LANES), F32)
        gate = jnp.zeros((GROUP, LANES), F32)
        for k in range(TOP):
            hit = tiles[k : k + 1, :] == expert_line
            hits = hits + jnp.where(hit, 1.0, 0.0)
            gate = gate + jnp.where(hit, tiles[TOP + k : TOP + k + 1, :], 0.0)
        count = dot(hits, earlier, (1, 0))
        wanted = (cube_row >> 1) == cube_source
        turn = (cube_row & 1).astype(F32)
        chosen = jnp.where(
            wanted & (jnp.broadcast_to(count[:, None, :], cube) == turn),
            jnp.broadcast_to(hits[:, None, :], cube),
            0.0,
        )
        pb[b] = chosen.reshape(SLOTS, LANES).astype(BF16)
        weight = jnp.sum(chosen * gate[:, None, :], axis=2, keepdims=True)
        sel[b * GROUP : (b + 1) * GROUP, :, 2 * D :] = lane_block(weight, cube)

    def pick(b, buf, offset):
        take = pb[b][:, : 4 * TOKS]

        @pl.loop(0, D // TILE)
        def _(i):
            block = buf[4 * b : 4 * b + 4, :, columns(i)].reshape(4 * TOKS, TILE)
            got = dot(take, block, (1, 0)).astype(BF16)
            where = pl.ds(pl.multiple_of(offset + i * TILE, TILE), TILE)
            sel[b * GROUP : (b + 1) * GROUP, :, where] = got.reshape(GROUP, 4 * PAIR, TILE)

    def exchange(b, src, dst, sem):
        copies = []
        for o in range(1, GROUP):
            m = (me + o) % GROUP
            copies.append(
                send(src.at[b * GROUP + m], dst.at[b * GROUP + me], "expert", member(m))
            )
        own = pltpu.make_async_copy(src.at[b * GROUP + me], dst.at[b * GROUP + me], sem)
        own.start()
        return copies, own

    def arrive(exchanged):
        for copy in exchanged[0]:
            copy.wait_recv()
        exchanged[1].wait()

    out_rows = {}
    for s in range(2, HALF + 1):
        ring_send(s)
        if s >= 3:
            b = (s - 3) // 2
            if s % 2:
                choose(b)
                pick(b, gx, 0)
            else:
                pick(b, gc, D)
                out_rows[b] = exchange(b, sel, rows, local_sem.at[2 + b])
        if s == 5:
            pass_weights()
    last = BATCHES - 1
    for name, way in (("m", 1), ("x", 1), ("c", -1)):
        ring[name, way, HALF].wait_recv()
    for name, way in (("m", -1), ("x", -1), ("c", 1)):
        ring[name, way, HALF - 1].wait_recv()
    choose(last)
    pick(last, gx, 0)
    pick(last, gc, D)
    out_rows[last] = exchange(last, sel, rows, local_sem.at[2 + last])
    for b in range(BATCHES):
        arrive(out_rows[b])

    def take_rows(offset):
        return rows[:, :, pl.ds(pl.multiple_of(offset, TILE), TILE)].reshape(ROWS, TILE)

    def first_products(slot, first):
        gate_up = dot(take_rows(slot * SHARD), wgf[slot], (1, 0))
        back = dot(take_rows(D + slot * SHARD), wdf[slot], (1, 0))
        if first:
            pre[...] = gate_up
            ub[...] = back
        else:
            pre[...] += gate_up
            ub[...] += back

    for copy in keep:
        copy.wait()
    first_products(x, True)
    for h in range(2):
        for i in range(2):
            to_right[i, h].wait_recv() if h else None
            to_left[i, 1 - h].wait_recv() if h else None
    first_products(left, False)
    first_products(right, False)
    for i in range(2):
        on_right[i].wait_recv()
        on_left[i].wait_recv()
    first_products((x + 2) % NX, False)

    step_rows = 32

    @pl.loop(0, ROWS // step_rows)
    def _(i):
        at = pl.ds(pl.multiple_of(i * step_rows, step_rows), step_rows)
        blocks = pl.ds(i * (step_rows // 8), step_rows // 8)
        gate_pre = pre[at, :FFW]
        up_pre = pre[at, FFW:]
        back = ub[at, :]
        weight = jnp.sum(
            rows[blocks, :, 2 * D :].astype(F32).reshape(step_rows, LANES), axis=1, keepdims=True
        )
        sigmoid_gate = jax.nn.sigmoid(gate_pre)
        activation = gate_pre * sigmoid_gate
        hidden = activation * up_pre
        hidden_grad = weight * back
        hs[at, :] = (weight * hidden).astype(BF16)
        pair[at, :FFW] = (
            hidden_grad * up_pre * (sigmoid_gate * (1.0 + gate_pre * (1.0 - sigmoid_gate)))
        ).astype(BF16)
        pair[at, FFW:] = (hidden_grad * activation).astype(BF16)
        score = jnp.sum(hidden * back, axis=1, keepdims=True)
        ob[blocks, :, 2 * D :] = lane_block(score, (step_rows, LANES)).reshape(
            step_rows // 8, 8, LANES
        )

    def weight_grads(o):
        slot = (x + o) % NX
        gp_gu[o] = dot(take_rows(slot * SHARD), pair[...], (0, 0)).astype(BF16)
        gp_d[o] = dot(take_rows(D + slot * SHARD), hs[...], (0, 0)).astype(BF16)

    grads = ((gp_gu, x2_gu, x1_gu), (gp_d, x2_d, x1_d))
    weight_grads(2)
    far_right, far_left, near = [], [], []
    for gp, x2, x1 in grads:
        far_right.append(send(gp.at[2, halves[0]], x2.at[0], "dp", right))
        far_left.append(send(gp.at[2, halves[1]], x2.at[1], "dp", left))

    @pl.loop(0, NX)
    def _(i):
        out = dot(hs[...], wdf[i], (1, 1)).astype(BF16)
        ob[:, :, columns(i)] = out.reshape(ROWS // 8, 8, TILE)
        back = dot(pair[...], wgf[i], (1, 1)).astype(BF16)
        where = pl.ds(pl.multiple_of(D + i * TILE, TILE), TILE)
        ob[:, :, where] = back.reshape(ROWS // 8, 8, TILE)

    back_rows = {}
    for b in reversed(range(BATCHES)):
        back_rows[b] = exchange(b, ob, cb, local_sem.at[2 + BATCHES + b])
    weight_grads(1)
    weight_grads(3)
    for gp, x2, x1 in grads:
        near.append(send(gp.at[1, halves[1]], x1.at[0, halves[1]], "dp", right))
        near.append(send(gp.at[3, halves[0]], x1.at[1, halves[0]], "dp", left))
    weight_grads(0)

    def pass_grads():
        for i, (gp, x2, x1) in enumerate(grads):
            far_right[i].wait_recv()
            gp[1, halves[0], :] = (gp[1, halves[0], :].astype(F32) + x2[0].astype(F32)).astype(BF16)
            near.append(send(gp.at[1, halves[0]], x1.at[0, halves[0]], "dp", right))
            far_left[i].wait_recv()
            gp[3, halves[1], :] = (gp[3, halves[1], :].astype(F32) + x2[1].astype(F32)).astype(BF16)
            near.append(send(gp.at[3, halves[1]], x1.at[1, halves[1]], "dp", left))

    def combine(b):
        arrive(back_rows[b])
        take = pb[b]

        @pl.loop(0, 2 * D // TILE)
        def _(i):
            got = cb[b * GROUP : (b + 1) * GROUP, :, columns(i)].reshape(SLOTS, TILE)
            total = dot(take, got, (0, 0))
            part[4 * b : 4 * b + 4, :, columns(i)] = total[: 4 * TOKS].reshape(4, TOKS, TILE)

        score = jnp.sum(
            cb[b * GROUP : (b + 1) * GROUP, :, 2 * D :].astype(F32), axis=2, keepdims=True
        )
        spread = jnp.sum(take.astype(F32).reshape(cube) * score, axis=1)
        tiles = comb[b]
        total = jnp.zeros((TOP, LANES), F32)
        for m in range(GROUP):
            hit = tiles[:TOP] == expert_line[m : m + 1, :]
            total = total + jnp.where(hit, spread[m : m + 1, :], 0.0)
        ggp[4 * b] = total
        for j in range(1, 4):
            ggp[4 * b + j] = pltpu.roll(total, LANES - TOKS * j, 1)

    going = {}

    def flow(name, way, q, buf, take, top):
        if q < top:
            going[name, way, q + 1].wait_recv()
            value = buf[q].astype(F32) + take(POS[q if way < 0 else (NZ - q) % NZ])
        else:
            value = take(POS[q if way < 0 else (NZ - q) % NZ])
        buf[q] = value.astype(buf.dtype)
        going[name, way, q] = send(
            buf.at[q], buf.at[q - 1], "expert", down if way < 0 else up
        )

    def mixed_part(p):
        return part[p, :, :D]

    def token_part(p):
        return part[p, :, D:]

    def gate_part(p):
        return ggp[p]

    combine(last)
    for k in range(1, HALF + 1):
        q = HALF + 1 - k
        flow("m", -1, q, dm, mixed_part, HALF)
        flow("t", 1, q, ud, token_part, HALF)
        flow("g", -1, q, dg, gate_part, HALF)
        if k > 1:
            flow("m", 1, q, um, mixed_part, HALF - 1)
            flow("t", -1, q, dd, token_part, HALF - 1)
            flow("g", 1, q, ug, gate_part, HALF - 1)
        if k % 2 == 0 and k < HALF:
            combine(last - k // 2)
        if k == 3:
            pass_grads()

    for way in (-1, 1):
        for name in ("m", "t", "g"):
            going[name, way, 1].wait_recv()
    home = POS[0]
    mixed[...] = (part[home, :, :D] + dm[0].astype(F32) + um[0].astype(F32)).astype(BF16)
    gtok[...] = (part[home, :, D:] + dd[0].astype(F32) + ud[0].astype(F32)).astype(BF16)
    gg[...] = ggp[home] + dg[0] + ug[0]
    for copy in near:
        copy.wait_recv()
    for (gp, x2, x1), out in zip(grads, (ggu, gd)):
        out[0] = (gp[0].astype(F32) + x1[0].astype(F32) + x1[1].astype(F32)).astype(BF16)
    for copy in started:
        copy.wait_send()


def body(tokens, route_ids, gates, cotangent, w_gate_up, w_down):
    pad = ((0, 0), (0, LANES - TOKS))
    meta = jnp.concatenate(
        [jnp.pad(route_ids.T.astype(F32) + 1.0, pad), jnp.pad(gates.T, pad)], axis=0
    )
    vmem = pl.BlockSpec(memory_space=pltpu.VMEM)
    out = pl.pallas_call(
        kernel,
        out_shape=(
            jax.ShapeDtypeStruct((TOKS, D), BF16),
            jax.ShapeDtypeStruct((TOKS, D), BF16),
            jax.ShapeDtypeStruct((TOP, LANES), F32),
            jax.ShapeDtypeStruct((1, SHARD, 2 * FFW), BF16),
            jax.ShapeDtypeStruct((1, SHARD, FFW), BF16),
        ),
        in_specs=[vmem] * 5,
        out_specs=[vmem] * 5,
        scratch_shapes=[
            pltpu.VMEM((NZ, TOKS, D), BF16),
            pltpu.VMEM((NZ, TOKS, D), BF16),
            pltpu.VMEM((NZ, 2 * TOP, LANES), F32),
            pltpu.VMEM((BATCHES, 2 * TOP, LANES), F32),
            pltpu.VMEM((BATCHES, SLOTS, LANES), BF16),
            pltpu.VMEM((ROWS // 8, 8, WIDE), BF16),
            pltpu.VMEM((ROWS // 8, 8, WIDE), BF16),
            pltpu.VMEM((NX, SHARD, 2 * FFW), BF16),
            pltpu.VMEM((NX, SHARD, FFW), BF16),
            pltpu.VMEM((ROWS, 2 * FFW), F32),
            pltpu.VMEM((ROWS, FFW), F32),
            pltpu.VMEM((ROWS, FFW), BF16),
            pltpu.VMEM((ROWS, 2 * FFW), BF16),
            pltpu.VMEM((ROWS // 8, 8, WIDE), BF16),
            pltpu.VMEM((ROWS // 8, 8, WIDE), BF16),
            pltpu.VMEM((NZ, TOKS, 2 * D), F32),
            pltpu.VMEM((NZ, TOP, LANES), F32),
            pltpu.VMEM((HALF + 1, TOKS, D), BF16),
            pltpu.VMEM((HALF, TOKS, D), BF16),
            pltpu.VMEM((HALF, TOKS, D), BF16),
            pltpu.VMEM((HALF + 1, TOKS, D), BF16),
            pltpu.VMEM((HALF + 1, TOP, LANES), F32),
            pltpu.VMEM((HALF, TOP, LANES), F32),
            pltpu.VMEM((NX, SHARD, 2 * FFW), BF16),
            pltpu.VMEM((NX, SHARD, FFW), BF16),
            pltpu.VMEM((2, SHARD // 2, 2 * FFW), BF16),
            pltpu.VMEM((2, SHARD // 2, FFW), BF16),
            pltpu.VMEM((2, SHARD, 2 * FFW), BF16),
            pltpu.VMEM((2, SHARD, FFW), BF16),
            pltpu.SemaphoreType.DMA((N_SEM,)),
            pltpu.SemaphoreType.DMA((N_SEM,)),
            pltpu.SemaphoreType.DMA((2 + 2 * BATCHES,)),
        ],
        compiler_params=pltpu.CompilerParams(
            collective_id=0, has_side_effects=True, vmem_limit_bytes=60 * 1024 * 1024
        ),
        name="routed_layer",
    )(tokens, cotangent, meta, w_gate_up, w_down)
    mixed, grad_tokens, grad_gates, grad_gate_up, grad_down = out
    return mixed, grad_tokens, grad_gates[:, :TOKS].T, grad_gate_up, grad_down


def solution(mesh):
    rows_spec = P(("expert", "dp"), None)
    weight_spec = P("expert", "dp", None)
    return jax.shard_map(
        body,
        mesh=mesh,
        in_specs=(rows_spec, rows_spec, rows_spec, rows_spec, weight_spec, weight_spec),
        out_specs=(rows_spec, rows_spec, rows_spec, weight_spec, weight_spec),
        check_vma=False,
    )
```

profile of v0, /device:TPU:2, one launch (start us, length us, event | category | flops | bytes accessed | tf_op | source)
XLA Modules:
  0.0 128.3 jit_solution(17243167162944589680)
XLA Ops:
  0.6 0.0 copy-start.3
  0.6 0.7 add_bitcast_fusion
  1.3 0.0 copy-done.3
  1.3 0.6 select_maximum_fusion.meta
  1.9 120.0 %routed_layer.1 = (bf16[24,2048]{1,0:T(8,128)(2,1)}, bf16[24,2048]{1,0:T(8,128)(2,1)}, f32[8,128]{1,0:T(8,128)}, bf16[1,512,768]{2,1,0:T(8,128)(2,1)}, bf16[1,512,384]{2,1,0:T(8,128)(2,1)}) custom-call(bf16[24,2048]{1,0:T(8,128)(2,1)} %tok.1, bf16[24,2048]{1,0:T(8,128)(2,1)} %cot.1, f32[16,128]{1,0:T(8,128)} %select_maximum_fusion.meta, ...), custom_call_target="tpu_custom_call" | custom-call | tf_op jit(solution)/shard_map/routed_layer/pallas_call | solution.py:420
  121.9 0.0 copy-start.2
  121.9 0.7 copy-done.2
  122.6 0.6 slice_bitcast_fusion
  123.2 0.0 copy-start.1
  123.2 1.6 %copy.15 = bf16[24,2048]{1,0:T(8,128)(2,1)} copy(bf16[24,2048]{1,0:T(8,128)(2,1)} %get-tuple-element.20) | data formatting | bytes 196608
  124.8 0.0 copy-done.1
  124.8 0.6 copy.16
  125.4 0.0 copy-start
  125.4 2.1 %copy.17 = bf16[1,512,768]{2,1,0:T(8,128)(2,1)} copy(bf16[1,512,768]{2,1,0:T(8,128)(2,1)} %get-tuple-element.23) | data formatting | bytes 1572864
  127.5 0.0 copy-done
  127.5 0.7 copy.18
Async XLA Ops:
  0.6 0.7 copy-start.3
  121.9 0.7 copy-start.2
  123.2 1.6 %copy-start.1 = (bf16[24,2048]{1,0:T(8,128)(2,1)S(1)}, bf16[24,2048]{1,0:T(8,128)(2,1)}, u32[]{:S(2)}) copy-start(bf16[24,2048]{1,0:T(8,128)(2,1)} %get-tuple-element.21) | copy-start | bytes 294916
  125.4 2.1 %copy-start = (bf16[1,512,384]{2,1,0:T(8,128)(2,1)S(1)}, bf16[1,512,384]{2,1,0:T(8,128)(2,1)}, u32[]{:S(2)}) copy-start(bf16[1,512,384]{2,1,0:T(8,128)(2,1)} %get-tuple-element.24) | copy-start | bytes 1179652
where the time goes:
time: 129 us; the launch traced here: 128 us
  Pallas kernels  120 us (93%)
  local copies, waits for them, and re-layouts  6.35 us (5%)
  other arithmetic  1.3 us (1%)
    pallas_call x1, Pallas kernels, body(): pl.pallas_call(kernel, out_shape=(jax.ShapeDtypeStruct((TOKS, D), BF16),...  120 us
    unnamed x12, local copies, waits for them, and re-layouts  5.76 us

commit v1 on v0

v1 whole, which is shorter than its diff:
```python
import jax
import jax.numpy as jnp
from jax import lax
from jax.experimental import pallas as pl
from jax.experimental.pallas import tpu as pltpu
from jax.sharding import PartitionSpec as P

NX, NY, NZ, NC = 4, 4, 16, 2
GROUP = NY * NC
HALF = NZ // 2
BATCHES = NZ // 4
PAIR = 2
TOKS = 24
TOP = 8
D = 2048
FFW = 384
LANES = 128
TILE = 512
NEXT = D + LANES
WIDE = D + NEXT
SHARD = D // NX
SLOTS = GROUP * 4 * PAIR
ROWS = BATCHES * SLOTS
N_SEM = 296
F32 = jnp.float32
BF16 = jnp.bfloat16


def positions():
    order = []
    for b in range(BATCHES):
        s = 2 * b + 1
        order += [s, NZ - s, s + 1, NZ - s - 1 if s + 1 < HALF else 0]
    return {d: i for i, d in enumerate(order)}


POS = positions()


def dot(a, b, contract):
    return lax.dot_general(a, b, ((contract[:1], contract[1:]), ((), ())), preferred_element_type=F32)


def columns(i, start=0):
    return pl.ds(pl.multiple_of(start + i * TILE, LANES), TILE)


def three_parts(v):
    high = v.astype(BF16).astype(F32)
    rest = v - high
    middle = rest.astype(BF16).astype(F32)
    return high, middle, rest - middle


def lane_block(v, shape):
    high, middle, low = three_parts(v)
    lane = lax.broadcasted_iota(jnp.int32, shape, len(shape) - 1)
    return jnp.where(
        lane == 0, high, jnp.where(lane == 1, middle, jnp.where(lane == 2, low, 0.0))
    ).astype(BF16)


def kernel(
    tok, cot, ids, gates, wg, wd,
    mixed, gtok, gg, ggu, gd,
    gx, gc, mb, comb, pb, sel, rows, wgf, wdf, pre, ub, gb, hs, pair, ob, cb,
    pm, pt, ggp, dm, um, dd, ud, dg, ug, gp_gu, gp_d, x2_gu, x2_d, x1_gu, x1_d,
    send_sem, recv_sem, local_sem,
):
    e = lax.axis_index("expert")
    x = lax.axis_index("dp")
    plane = NZ * NC
    y = e // plane
    z = (e // NC) % NZ
    c = e % NC
    me = y * NC + c
    up = y * plane + ((z + 1) % NZ) * NC + c
    down = y * plane + ((z + NZ - 1) % NZ) * NC + c
    right = (x + 1) % NX
    left = (x + NX - 1) % NX

    def member(m):
        return (m // NC) * plane + z * NC + m % NC

    barrier = pltpu.get_barrier_semaphore()
    peers = [("expert", up), ("expert", down), ("dp", right), ("dp", left)]
    peers += [("expert", member((me + o) % GROUP)) for o in range(1, GROUP)]
    for axis, target in peers:
        pl.semaphore_signal(
            barrier, inc=1, device_id={axis: target}, device_id_type=pl.DeviceIdType.MESH
        )
    pl.semaphore_wait(barrier, len(peers))

    started = []

    def send(src, dst, axis, target):
        i = len(started)
        copy = pltpu.make_async_remote_copy(
            src_ref=src,
            dst_ref=dst,
            send_sem=send_sem.at[i],
            recv_sem=recv_sem.at[i],
            device_id={axis: target},
            device_id_type=pl.DeviceIdType.MESH,
        )
        copy.start()
        started.append(copy)
        return copy

    halves = [pl.ds(h * (SHARD // 2), SHARD // 2) for h in range(2)]
    half_cols = [pl.ds(h * (D // 2), D // 2) for h in range(2)]
    home = POS[0]
    mb[home] = jnp.zeros((2 * TOP, LANES), F32)
    mb[home, :TOP, :TOKS] = ids[...].astype(F32) + 1.0
    mb[home, TOP:, :TOKS] = gates[...]
    chunks = [("m", 0, mb.at[home], mb)]
    chunks += [("x", h, tok, gx) for h in range(2)] + [("c", h, cot, gc) for h in range(2)]
    ring = {}

    def ring_send(s):
        for name, h, own, buf in chunks:
            for way, target in ((1, up), (-1, down)):
                if s > (HALF if (way < 0) == (name == "c") else HALF - 1):
                    continue
                src, dst = own, buf.at[POS[(way * s) % NZ]]
                if s > 1:
                    ring[name, h, way, s - 1].wait_recv()
                    src = buf.at[POS[(way * (s - 1)) % NZ]]
                if name != "m":
                    src, dst = src.at[:, half_cols[h]], dst.at[:, half_cols[h]]
                ring[name, h, way, s] = send(src, dst, "expert", target)

    def ring_wait(name):
        for h in range(1 if name == "m" else 2):
            ring[name, h, 1, HALF - (name == "c")].wait_recv()
            ring[name, h, -1, HALF - (name != "c")].wait_recv()

    ring_send(1)

    weights = ((wg, wgf), (wd, wdf))
    to_right, to_left = {}, {}
    for h in range(2):
        for i, (w, full) in enumerate(weights):
            to_right[i, h] = send(w.at[0, halves[h]], full.at[x, halves[h]], "dp", right)
            g = 1 - h
            to_left[i, g] = send(w.at[0, halves[g]], full.at[x, halves[g]], "dp", left)
    keep = [
        pltpu.make_async_copy(w.at[0], full.at[x], local_sem.at[i])
        for i, (w, full) in enumerate(weights)
    ]
    keep.append(pltpu.make_async_copy(tok, gx.at[home], local_sem.at[2]))
    keep.append(pltpu.make_async_copy(cot, gc.at[home], local_sem.at[3]))
    for copy in keep:
        copy.start()
    on_right, on_left = {}, {}

    def pass_weights():
        for i, (w, full) in enumerate(weights):
            to_right[i, 0].wait_recv()
            piece = full.at[left, halves[0]]
            on_right[i] = send(piece, piece, "dp", right)
            to_left[i, 1].wait_recv()
            piece = full.at[right, halves[1]]
            on_left[i] = send(piece, piece, "dp", left)


    lane = lax.broadcasted_iota(jnp.int32, (LANES, LANES), 1)
    line = lax.broadcasted_iota(jnp.int32, (LANES, LANES), 0)

    def source_of(index):
        total = jnp.zeros(index.shape, jnp.int32)
        for j in range(1, 5):
            total = total + jnp.where(index >= j * TOKS, 1, 0)
        return total

    earlier = jnp.where((line < lane) & (source_of(line) == source_of(lane)), 1.0, 0.0).astype(F32)
    member_line = lax.broadcasted_iota(jnp.int32, (GROUP, LANES), 0)
    expert_line = ((member_line >> 1) * plane + z * NC + (member_line & 1) + 1).astype(F32)
    cube = (GROUP, 4 * PAIR, LANES)
    cube_row = lax.broadcasted_iota(jnp.int32, cube, 1)
    cube_source = source_of(lax.broadcasted_iota(jnp.int32, cube, 2))

    def choose(b):
        tiles = mb[4 * b]
        for j in range(1, 4):
            tiles = tiles + pltpu.roll(mb[4 * b + j], TOKS * j, 1)
        comb[b] = tiles
        hits = jnp.zeros((GROUP, LANES), F32)
        gate = jnp.zeros((GROUP, LANES), F32)
        for k in range(TOP):
            hit = tiles[k : k + 1, :] == expert_line
            hits = hits + jnp.where(hit, 1.0, 0.0)
            gate = gate + jnp.where(hit, tiles[TOP + k : TOP + k + 1, :], 0.0)
        count = dot(hits, earlier, (1, 0))
        wanted = (cube_row >> 1) == cube_source
        turn = (cube_row & 1).astype(F32)
        chosen = jnp.where(
            wanted & (jnp.broadcast_to(count[:, None, :], cube) == turn),
            jnp.broadcast_to(hits[:, None, :], cube),
            0.0,
        )
        pb[b] = chosen.reshape(SLOTS, LANES).astype(BF16)
        weight = jnp.sum(chosen * gate[:, None, :], axis=2, keepdims=True)
        sel[b * GROUP : (b + 1) * GROUP, :, D:NEXT] = lane_block(weight, cube)

    def pick(b, buf, offset):
        take = pb[b][:, : 4 * TOKS]
        batch = slice(b * GROUP, (b + 1) * GROUP)
        weight = jnp.sum(sel[batch, :, D:NEXT].astype(F32), axis=2, keepdims=True)
        for i in range(D // TILE):
            block = buf[4 * b : 4 * b + 4, :, i * TILE : (i + 1) * TILE].reshape(4 * TOKS, TILE)
            got = dot(take, block, (1, 0)).reshape(GROUP, 4 * PAIR, TILE)
            if offset:
                got = got * weight
            sel[batch, :, offset + i * TILE : offset + (i + 1) * TILE] = got.astype(BF16)

    parts = (pl.ds(0, NEXT), pl.ds(NEXT, D))

    def exchange(b, src, dst, part, sem):
        copies = []
        for o in range(1, GROUP):
            m = (me + o) % GROUP
            copies.append(
                send(
                    src.at[b * GROUP + m, :, parts[part]],
                    dst.at[b * GROUP + me, :, parts[part]],
                    "expert",
                    member(m),
                )
            )
        own = pltpu.make_async_copy(
            src.at[b * GROUP + me, :, parts[part]],
            dst.at[b * GROUP + me, :, parts[part]],
            local_sem.at[sem],
        )
        own.start()
        return copies, own

    def arrive(exchanged):
        for copy in exchanged[0]:
            copy.wait_recv()
        exchanged[1].wait()

    out_rows = {}
    for s in range(2, HALF + 1):
        ring_send(s)
        if s >= 3:
            b = (s - 3) // 2
            if s % 2:
                choose(b)
                pick(b, gx, 0)
                out_rows[b, 0] = exchange(b, sel, rows, 0, 4 + 2 * b)
            else:
                pick(b, gc, NEXT)
                out_rows[b, 1] = exchange(b, sel, rows, 1, 5 + 2 * b)
        if s == 5:
            pass_weights()
    last = BATCHES - 1
    for copy in keep:
        copy.wait()
    ring_wait("m")
    choose(last)
    ring_wait("x")
    pick(last, gx, 0)
    out_rows[last, 0] = exchange(last, sel, rows, 0, 4 + 2 * last)
    ring_wait("c")
    pick(last, gc, NEXT)
    out_rows[last, 1] = exchange(last, sel, rows, 1, 5 + 2 * last)
    n_first = len(started)

    def take_rows(i, start=0):
        return rows[:, :, columns(i, start)].reshape(ROWS, TILE)

    def gate_up_product(slot, first):
        value = dot(take_rows(slot), wgf[slot], (1, 0))
        pre[...] = value if first else pre[...] + value

    def down_product(slot, first):
        value = dot(take_rows(slot, NEXT), wdf[slot], (1, 0))
        ub[...] = value if first else ub[...] + value

    for b in range(BATCHES):
        arrive(out_rows[b, 0])
    gate_up_product(x, True)
    for i in range(2):
        to_right[i, 1].wait_recv()
        to_left[i, 0].wait_recv()
    gate_up_product(left, False)
    gate_up_product(right, False)
    for i in range(2):
        on_right[i].wait_recv()
        on_left[i].wait_recv()
    gate_up_product((x + 2) % NX, False)
    for b in range(BATCHES):
        arrive(out_rows[b, 1])
    down_product(0, True)
    for i in range(1, NX):
        down_product(i, False)

    step_rows = 32

    @pl.loop(0, ROWS // step_rows)
    def _(i):
        at = pl.ds(pl.multiple_of(i * step_rows, step_rows), step_rows)
        blocks = pl.ds(i * (step_rows // 8), step_rows // 8)
        gate_pre = pre[at, :FFW]
        up_pre = pre[at, FFW:]
        back = ub[at, :]
        weight = jnp.sum(
            rows[blocks, :, D:NEXT].astype(F32).reshape(step_rows, LANES), axis=1, keepdims=True
        )
        sigmoid_gate = jax.nn.sigmoid(gate_pre)
        activation = gate_pre * sigmoid_gate
        hidden = activation * up_pre
        gb[at, :] = jnp.broadcast_to(weight, (step_rows, LANES))
        hs[at, :] = hidden.astype(BF16)
        pair[at, :FFW] = (
            back * up_pre * (sigmoid_gate * (1.0 + gate_pre * (1.0 - sigmoid_gate)))
        ).astype(BF16)
        pair[at, FFW:] = (back * activation).astype(BF16)
        score = jnp.sum(hidden * back, axis=1, keepdims=True)
        score = score / jnp.where(weight > 0.0, weight, 1.0)
        ob[blocks, :, D:NEXT] = lane_block(score, (step_rows, LANES)).reshape(
            step_rows // 8, 8, LANES
        )

    def send_back(b, part):
        return exchange(b, ob, cb, part, 4 + 2 * BATCHES + 2 * b + part)

    last = BATCHES - 1
    back_rows = {}
    scale = gb[:, :1]
    for i in range(NX):
        out = (dot(hs[...], wdf[i], (1, 1)) * scale).astype(BF16)
        ob[:, :, i * TILE : (i + 1) * TILE] = out.reshape(ROWS // 8, 8, TILE)
    back_rows[last, 0] = send_back(last, 0)
    for i in range(NX):
        back = dot(pair[...], wgf[i], (1, 1)).astype(BF16)
        ob[:, :, NEXT + i * TILE : NEXT + (i + 1) * TILE] = back.reshape(ROWS // 8, 8, TILE)
    back_rows[last, 1] = send_back(last, 1)

    def weight_grads(o):
        slot = (x + o) % NX
        gp_gu[o] = dot(take_rows(slot), pair[...], (0, 0)).astype(BF16)
        gp_d[o] = dot(take_rows(slot, NEXT), hs[...], (0, 0)).astype(BF16)

    grads = ((gp_gu, x2_gu, x1_gu), (gp_d, x2_d, x1_d))
    far_right, far_left, near = [], [], []

    def far_grads():
        weight_grads(2)
        for gp, x2, x1 in grads:
            far_right.append(send(gp.at[2, halves[0]], x2.at[0], "dp", right))
            far_left.append(send(gp.at[2, halves[1]], x2.at[1], "dp", left))

    def right_grads():
        weight_grads(1)
        for gp, x2, x1 in grads:
            near.append(send(gp.at[1, halves[1]], x1.at[0, halves[1]], "dp", right))

    def left_grads():
        weight_grads(3)
        for gp, x2, x1 in grads:
            near.append(send(gp.at[3, halves[0]], x1.at[1, halves[0]], "dp", left))

    def pass_grads():
        for i, (gp, x2, x1) in enumerate(grads):
            far_right[i].wait_recv()
            gp[1, halves[0], :] = (gp[1, halves[0], :].astype(F32) + x2[0].astype(F32)).astype(BF16)
            near.append(send(gp.at[1, halves[0]], x1.at[0, halves[0]], "dp", right))
            far_left[i].wait_recv()
            gp[3, halves[1], :] = (gp[3, halves[1], :].astype(F32) + x2[1].astype(F32)).astype(BF16)
            near.append(send(gp.at[3, halves[1]], x1.at[1, halves[1]], "dp", left))

    def combine(b, part):
        arrive(back_rows[b, part])
        take = pb[b]
        batch = slice(b * GROUP, (b + 1) * GROUP)
        start, total = ((0, pm), (NEXT, pt))[part]
        for i in range(D // TILE):
            got = cb[batch, :, start + i * TILE : start + (i + 1) * TILE].reshape(SLOTS, TILE)
            value = dot(take, got, (0, 0))[: 4 * TOKS].reshape(4, TOKS, TILE)
            total[4 * b : 4 * b + 4, :, i * TILE : (i + 1) * TILE] = value
        if part:
            return
        score = jnp.sum(cb[batch, :, D:NEXT].astype(F32), axis=2, keepdims=True)
        spread = jnp.sum(take.astype(F32).reshape(cube) * score, axis=1)
        tiles = comb[b]
        total = jnp.zeros((TOP, LANES), F32)
        for m in range(GROUP):
            hit = tiles[:TOP] == expert_line[m : m + 1, :]
            total = total + jnp.where(hit, spread[m : m + 1, :], 0.0)
        ggp[4 * b] = total
        for j in range(1, 4):
            ggp[4 * b + j] = pltpu.roll(total, LANES - TOKS * j, 1)

    going = {}

    def flow(name, way, q, buf, total, top, h=None):
        cols = slice(None) if h is None else slice(h * (D // 2), (h + 1) * (D // 2))
        value = total[POS[q if way < 0 else (NZ - q) % NZ], :, cols]
        if q < top:
            going[name, way, h, q + 1].wait_recv()
            value = value + buf[q, :, cols].astype(F32)
        buf[q, :, cols] = value.astype(buf.dtype)
        src, dst = buf.at[q], buf.at[q - 1]
        if h is not None:
            src, dst = src.at[:, half_cols[h]], dst.at[:, half_cols[h]]
        going[name, way, h, q] = send(src, dst, "expert", down if way < 0 else up)

    def step(k):
        q = HALF + 1 - k
        for h in range(2):
            flow("m", -1, q, dm, pm, HALF, h)
            if k > 1:
                flow("m", 1, q, um, pm, HALF - 1, h)
        flow("g", -1, q, dg, ggp, HALF)
        if k > 1:
            flow("g", 1, q, ug, ggp, HALF - 1)
        else:
            combine(last, 1)
        for h in range(2):
            flow("t", 1, q, ud, pt, HALF, h)
            if k > 1:
                flow("t", -1, q, dd, pt, HALF - 1, h)

    settled = []

    def settle(count):
        for copy in started[len(settled) : count]:
            copy.wait_send()
            settled.append(copy)

    far_grads()
    back_rows[last - 1, 0] = send_back(last - 1, 0)
    back_rows[last - 1, 1] = send_back(last - 1, 1)
    combine(last, 0)
    step(1)
    for b in reversed(range(last - 1)):
        back_rows[b, 0] = send_back(b, 0)
        back_rows[b, 1] = send_back(b, 1)
    right_grads()
    step(2)
    left_grads()
    combine(last - 1, 0)
    combine(last - 1, 1)
    step(3)
    weight_grads(0)
    settle(n_first)
    step(4)
    combine(last - 2, 0)
    combine(last - 2, 1)
    step(5)
    pass_grads()
    step(6)
    combine(last - 3, 0)
    combine(last - 3, 1)
    step(7)
    settle(len(started) - 60)
    step(8)

    for key, copy in going.items():
        if key[-1] == 1:
            copy.wait_recv()
    mixed[...] = (pm[home] + dm[0].astype(F32) + um[0].astype(F32)).astype(BF16)
    gtok[...] = (pt[home] + dd[0].astype(F32) + ud[0].astype(F32)).astype(BF16)
    gg[...] = ggp[home] + dg[0] + ug[0]
    for copy in near:
        copy.wait_recv()
    for (gp, x2, x1), out in zip(grads, (ggu, gd)):
        out[0] = (gp[0].astype(F32) + x1[0].astype(F32) + x1[1].astype(F32)).astype(BF16)
    settle(len(started))


def hand_over(m, t, g, u, d, m_out, t_out, g_out, u_out, d_out, mv, tv, uv, dv, sem, sem_out):
    arrays = ((u, uv, u_out), (d, dv, d_out), (m, mv, m_out), (t, tv, t_out))
    loads = [pltpu.make_async_copy(a, v, sem.at[i]) for i, (a, v, o) in enumerate(arrays)]
    for copy in loads:
        copy.start()
    g_out[...] = g[:, :TOKS]
    stores = []
    for i, (a, v, o) in enumerate(arrays):
        loads[i].wait()
        stores.append(pltpu.make_async_copy(v, o, sem_out.at[i]))
        stores[i].start()
    for copy in stores:
        copy.wait()


def body(tokens, route_ids, gates, cotangent, w_gate_up, w_down):
    vmem = pl.BlockSpec(memory_space=pltpu.VMEM)
    hbm = pl.BlockSpec(memory_space=pl.ANY)
    out = pl.pallas_call(
        kernel,
        out_shape=(
            jax.ShapeDtypeStruct((TOKS, D), BF16),
            jax.ShapeDtypeStruct((TOKS, D), BF16),
            jax.ShapeDtypeStruct((TOP, LANES), F32),
            jax.ShapeDtypeStruct((1, SHARD, 2 * FFW), BF16),
            jax.ShapeDtypeStruct((1, SHARD, FFW), BF16),
        ),
        in_specs=[hbm, hbm, vmem, vmem, hbm, hbm],
        out_specs=[vmem] * 5,
        scratch_shapes=[
            pltpu.VMEM((NZ, TOKS, D), BF16),
            pltpu.VMEM((NZ, TOKS, D), BF16),
            pltpu.VMEM((NZ, 2 * TOP, LANES), F32),
            pltpu.VMEM((BATCHES, 2 * TOP, LANES), F32),
            pltpu.VMEM((BATCHES, SLOTS, LANES), BF16),
            pltpu.VMEM((ROWS // 8, 8, WIDE), BF16),
            pltpu.VMEM((ROWS // 8, 8, WIDE), BF16),
            pltpu.VMEM((NX, SHARD, 2 * FFW), BF16),
            pltpu.VMEM((NX, SHARD, FFW), BF16),
            pltpu.VMEM((ROWS, 2 * FFW), F32),
            pltpu.VMEM((ROWS, FFW), F32),
            pltpu.VMEM((ROWS, LANES), F32),
            pltpu.VMEM((ROWS, FFW), BF16),
            pltpu.VMEM((ROWS, 2 * FFW), BF16),
            pltpu.VMEM((ROWS // 8, 8, WIDE), BF16),
            pltpu.VMEM((ROWS // 8, 8, WIDE), BF16),
            pltpu.VMEM((NZ, TOKS, D), F32),
            pltpu.VMEM((NZ, TOKS, D), F32),
            pltpu.VMEM((NZ, TOP, LANES), F32),
            pltpu.VMEM((HALF + 1, TOKS, D), BF16),
            pltpu.VMEM((HALF, TOKS, D), BF16),
            pltpu.VMEM((HALF, TOKS, D), BF16),
            pltpu.VMEM((HALF + 1, TOKS, D), BF16),
            pltpu.VMEM((HALF + 1, TOP, LANES), F32),
            pltpu.VMEM((HALF, TOP, LANES), F32),
            pltpu.VMEM((NX, SHARD, 2 * FFW), BF16),
            pltpu.VMEM((NX, SHARD, FFW), BF16),
            pltpu.VMEM((2, SHARD // 2, 2 * FFW), BF16),
            pltpu.VMEM((2, SHARD // 2, FFW), BF16),
            pltpu.VMEM((2, SHARD, 2 * FFW), BF16),
            pltpu.VMEM((2, SHARD, FFW), BF16),
            pltpu.SemaphoreType.DMA((N_SEM,)),
            pltpu.SemaphoreType.DMA((N_SEM,)),
            pltpu.SemaphoreType.DMA((4 + 4 * BATCHES,)),
        ],
        compiler_params=pltpu.CompilerParams(
            collective_id=0, has_side_effects=True, vmem_limit_bytes=60 * 1024 * 1024
        ),
        name="routed_layer",
    )(tokens, cotangent, route_ids.T, gates.T, w_gate_up, w_down)
    specs = [hbm, hbm, vmem, hbm, hbm]
    mixed, grad_tokens, grad_gates, grad_gate_up, grad_down = pl.pallas_call(
        hand_over,
        out_shape=(
            jax.ShapeDtypeStruct((TOKS, D), BF16),
            jax.ShapeDtypeStruct((TOKS, D), BF16),
            jax.ShapeDtypeStruct((TOP, TOKS), F32),
            jax.ShapeDtypeStruct((1, SHARD, 2 * FFW), BF16),
            jax.ShapeDtypeStruct((1, SHARD, FFW), BF16),
        ),
        in_specs=specs,
        out_specs=specs,
        scratch_shapes=[
            pltpu.VMEM((TOKS, D), BF16),
            pltpu.VMEM((TOKS, D), BF16),
            pltpu.VMEM((1, SHARD, 2 * FFW), BF16),
            pltpu.VMEM((1, SHARD, FFW), BF16),
            pltpu.SemaphoreType.DMA((4,)),
            pltpu.SemaphoreType.DMA((4,)),
        ],
        name="hand_over",
    )(*out)
    return mixed, grad_tokens, grad_gates.T, grad_gate_up, grad_down


def solution(mesh):
    rows_spec = P(("expert", "dp"), None)
    weight_spec = P("expert", "dp", None)
    return jax.shard_map(
        body,
        mesh=mesh,
        in_specs=(rows_spec, rows_spec, rows_spec, rows_spec, weight_spec, weight_spec),
        out_specs=(rows_spec, rows_spec, rows_spec, weight_spec, weight_spec),
        check_vma=False,
    )
```

time: 129 us -> 115 us (0.89)
  the two profiles are of different devices: /device:TPU:2 before, /device:TPU:1 now
where the time goes in v1:
time: 115 us
  Pallas kernels  114 us (99%)
    pallas_call x1, Pallas kernels, body(): pl.pallas_call(kernel, out_shape=(jax.ShapeDtypeStruct((TOKS, D), BF16),...  111 us
    pallas_call x1, Pallas kernels, body(): pl.pallas_call(hand_over, out_shape=(jax.ShapeDtypeStruct((TOKS, D), BF16...  3.54 us

profile of v1, /device:TPU:1, one launch (start us, length us, event | category | flops | bytes accessed | tf_op | source)
XLA Modules:
  0.0 114.9 jit_solution(6807700861251251420)
XLA Ops:
  0.6 110.8 %routed_layer.1 = (bf16[24,2048]{1,0:T(8,128)(2,1)}, bf16[24,2048]{1,0:T(8,128)(2,1)}, f32[8,128]{1,0:T(8,128)}, bf16[1,512,768]{2,1,0:T(8,128)(2,1)}, bf16[1,512,384]{2,1,0:T(8,128)(2,1)}) custom-call(bf16[24,2048]{1,0:T(8,128)(2,1)} %tok.1, bf16[24,2048]{1,0:T(8,128)(2,1)} %cot.1, s32[8,24]{1,0:T(8,128)} %bitcast.3, f32[8,24]{1,0:T(8,128)} %bitcast.4, ...), custom_call_target="tpu_custom_call" | custom-call | tf_op jit(solution)/shard_map/routed_layer/pallas_call | solution.py:493
  111.4 3.5 %hand_over.1 = (bf16[24,2048]{1,0:T(8,128)(2,1)}, bf16[24,2048]{1,0:T(8,128)(2,1)}, f32[8,24]{1,0:T(8,128)}, bf16[1,512,768]{2,1,0:T(8,128)(2,1)}, bf16[1,512,384]{2,1,0:T(8,128)(2,1)}) custom-call(bf16[24,2048]{1,0:T(8,128)(2,1)} %get-tuple-element.15.m, bf16[24,2048]{1,0:T(8,128)(2,1)} %get-tuple-element.16.t, f32[8,128]{1,0:T(8,128)} %get-tuple-element.17.g, ...), custom_call_target="tpu_custom_call" | custom-call | tf_op jit(solution)/shard_map/hand_over/pallas_call | solution.py:546

commit v2 on v1

--- a/solution.py
+++ b/solution.py
@@ -64,7 +64,7 @@
     tok, cot, ids, gates, wg, wd,
     mixed, gtok, gg, ggu, gd,
     gx, gc, mb, comb, pb, sel, rows, wgf, wdf, pre, ub, gb, hs, pair, ob, cb,
-    pm, pt, ggp, dm, um, dd, ud, dg, ug, gp_gu, gp_d, x2_gu, x2_d, x1_gu, x1_d,
+    pm, pt, ggp, dm, um, dd, ud, dg, ug, gp_gu, gp_d, x2_gu, x2_d, x1_gu, x1_d, fm, ft,
     send_sem, recv_sem, local_sem,
 ):
     e = lax.axis_index("expert")
@@ -113,14 +113,17 @@
     mb[home] = jnp.zeros((2 * TOP, LANES), F32)
     mb[home, :TOP, :TOKS] = ids[...].astype(F32) + 1.0
     mb[home, TOP:, :TOKS] = gates[...]
-    chunks = [("m", 0, mb.at[home], mb)]
-    chunks += [("x", h, tok, gx) for h in range(2)] + [("c", h, cot, gc) for h in range(2)]
+    chunks = [("x", 0, tok, gx), ("x", 1, tok, gx), ("m", 0, mb.at[home], mb)]
+    chunks += [("c", 0, cot, gc), ("c", 1, cot, gc)]
     ring = {}
+
+    def reach(way, h):
+        return HALF if (way > 0) == (h == 0) else HALF - 1
 
     def ring_send(s):
         for name, h, own, buf in chunks:
             for way, target in ((1, up), (-1, down)):
-                if s > (HALF if (way < 0) == (name == "c") else HALF - 1):
+                if s > reach(way, h):
                     continue
                 src, dst = own, buf.at[POS[(way * s) % NZ]]
                 if s > 1:
@@ -132,8 +135,8 @@
 
     def ring_wait(name):
         for h in range(1 if name == "m" else 2):
-            ring[name, h, 1, HALF - (name == "c")].wait_recv()
-            ring[name, h, -1, HALF - (name != "c")].wait_recv()
+            ring[name, h, 1, reach(1, h)].wait_recv()
+            ring[name, h, -1, reach(-1, h)].wait_recv()
 
     ring_send(1)
 
@@ -327,18 +330,6 @@
     def send_back(b, part):
         return exchange(b, ob, cb, part, 4 + 2 * BATCHES + 2 * b + part)
 
-    last = BATCHES - 1
-    back_rows = {}
-    scale = gb[:, :1]
-    for i in range(NX):
-        out = (dot(hs[...], wdf[i], (1, 1)) * scale).astype(BF16)
-        ob[:, :, i * TILE : (i + 1) * TILE] = out.reshape(ROWS // 8, 8, TILE)
-    back_rows[last, 0] = send_back(last, 0)
-    for i in range(NX):
-        back = dot(pair[...], wgf[i], (1, 1)).astype(BF16)
-        ob[:, :, NEXT + i * TILE : NEXT + (i + 1) * TILE] = back.reshape(ROWS // 8, 8, TILE)
-    back_rows[last, 1] = send_back(last, 1)
-
     def weight_grads(o):
         slot = (x + o) % NX
         gp_gu[o] = dot(take_rows(slot), pair[...], (0, 0)).astype(BF16)
@@ -396,33 +387,32 @@
 
     going = {}
 
-    def flow(name, way, q, buf, total, top, h=None):
-        cols = slice(None) if h is None else slice(h * (D // 2), (h + 1) * (D // 2))
-        value = total[POS[q if way < 0 else (NZ - q) % NZ], :, cols]
-        if q < top:
+    def flow(name, way, k, buf, total, h=0):
+        q = HALF + 1 - k
+        if q > reach(-way, h):
+            return
+        cols = slice(None) if name == "g" else slice(h * (D // 2), (h + 1) * (D // 2))
+        value = total[POS[(-way * q) % NZ], :, cols]
+        if q < reach(-way, h):
             going[name, way, h, q + 1].wait_recv()
             value = value + buf[q, :, cols].astype(F32)
         buf[q, :, cols] = value.astype(buf.dtype)
         src, dst = buf.at[q], buf.at[q - 1]
-        if h is not None:
+        if name != "g":
             src, dst = src.at[:, half_cols[h]], dst.at[:, half_cols[h]]
         going[name, way, h, q] = send(src, dst, "expert", down if way < 0 else up)
 
-    def step(k):
-        q = HALF + 1 - k
+    def mixed_step(k):
         for h in range(2):
-            flow("m", -1, q, dm, pm, HALF, h)
-            if k > 1:
-                flow("m", 1, q, um, pm, HALF - 1, h)
-        flow("g", -1, q, dg, ggp, HALF)
-        if k > 1:
-            flow("g", 1, q, ug, ggp, HALF - 1)
-        else:
-            combine(last, 1)
+            flow("m", -1, k, dm, pm, h)
+            flow("m", 1, k, um, pm, h)
+
+    def token_step(k):
+        flow("g", -1, k, dg, ggp)
+        flow("g", 1, k, ug, ggp)
         for h in range(2):
-            flow("t", 1, q, ud, pt, HALF, h)
-            if k > 1:
-                flow("t", -1, q, dd, pt, HALF - 1, h)
+            flow("t", -1, k, dd, pt, h)
+            flow("t", 1, k, ud, pt, h)
 
     settled = []
 
@@ -431,55 +421,94 @@
             copy.wait_send()
             settled.append(copy)
 
+    back_rows = {}
+    scale = gb[:, :1]
+    for i in range(NX):
+        out = (dot(hs[...], wdf[i], (1, 1)) * scale).astype(BF16)
+        ob[:, :, i * TILE : (i + 1) * TILE] = out.reshape(ROWS // 8, 8, TILE)
+    back_rows[3, 0] = send_back(3, 0)
     far_grads()
-    back_rows[last - 1, 0] = send_back(last - 1, 0)
-    back_rows[last - 1, 1] = send_back(last - 1, 1)
-    combine(last, 0)
-    step(1)
-    for b in reversed(range(last - 1)):
-        back_rows[b, 0] = send_back(b, 0)
-        back_rows[b, 1] = send_back(b, 1)
+    for i in range(NX):
+        back = dot(pair[...], wgf[i], (1, 1)).astype(BF16)
+        ob[:, :, NEXT + i * TILE : NEXT + (i + 1) * TILE] = back.reshape(ROWS // 8, 8, TILE)
+    back_rows[3, 1] = send_back(3, 1)
+    back_rows[2, 0] = send_back(2, 0)
+    back_rows[2, 1] = send_back(2, 1)
+    combine(3, 0)
+    mixed_step(1)
+    combine(3, 1)
+    token_step(1)
+    back_rows[1, 0] = send_back(1, 0)
+    back_rows[1, 1] = send_back(1, 1)
     right_grads()
-    step(2)
+    mixed_step(2)
     left_grads()
-    combine(last - 1, 0)
-    combine(last - 1, 1)
-    step(3)
+    token_step(2)
+    combine(2, 0)
+    mixed_step(3)
+    combine(2, 1)
+    token_step(3)
+    back_rows[0, 0] = send_back(0, 0)
+    back_rows[0, 1] = send_back(0, 1)
+    mixed_step(4)
     weight_grads(0)
+    token_step(4)
+    combine(1, 0)
+    pass_grads()
+    mixed_step(5)
+    combine(1, 1)
+    token_step(5)
+    settle(n_first // 2)
+    mixed_step(6)
     settle(n_first)
-    step(4)
-    combine(last - 2, 0)
-    combine(last - 2, 1)
-    step(5)
-    pass_grads()
-    step(6)
-    combine(last - 3, 0)
-    combine(last - 3, 1)
-    step(7)
-    settle(len(started) - 60)
-    step(8)
-
+    token_step(6)
+    combine(0, 0)
+    mixed_step(7)
+    combine(0, 1)
+    token_step(7)
+    settle(len(started) - 80)
+    mixed_step(8)
+    settle(len(started) - 40)
+    token_step(8)
+
+    leaving = []
+
+    def leave(src, dst):
+        leaving.append(pltpu.make_async_copy(src, dst, local_sem.at[len(leaving)]))
+        leaving[-1].start()
+
+    for copy in near:
+        copy.wait_recv()
+    for (gp, x2, x1), out in zip(grads, (ggu, gd)):
+        for at in halves:
+            gp[0, at, :] = (
+                gp[0, at, :].astype(F32) + x1[0, at, :].astype(F32) + x1[1, at, :].astype(F32)
+            ).astype(BF16)
+            leave(gp.at[0, at], out.at[0, at])
     for key, copy in going.items():
         if key[-1] == 1:
             copy.wait_recv()
-    mixed[...] = (pm[home] + dm[0].astype(F32) + um[0].astype(F32)).astype(BF16)
-    gtok[...] = (pt[home] + dd[0].astype(F32) + ud[0].astype(F32)).astype(BF16)
+    fm[...] = (pm[home] + dm[0].astype(F32) + um[0].astype(F32)).astype(BF16)
+    leave(fm, mixed)
+    ft[...] = (pt[home] + dd[0].astype(F32) + ud[0].astype(F32)).astype(BF16)
+    leave(ft, gtok)
     gg[...] = ggp[home] + dg[0] + ug[0]
-    for copy in near:
-        copy.wait_recv()
-    for (gp, x2, x1), out in zip(grads, (ggu, gd)):
-        out[0] = (gp[0].astype(F32) + x1[0].astype(F32) + x1[1].astype(F32)).astype(BF16)
     settle(len(started))
+    for copy in leaving:
+        copy.wait()
 
 
 def hand_over(m, t, g, u, d, m_out, t_out, g_out, u_out, d_out, mv, tv, uv, dv, sem, sem_out):
-    arrays = ((u, uv, u_out), (d, dv, d_out), (m, mv, m_out), (t, tv, t_out))
-    loads = [pltpu.make_async_copy(a, v, sem.at[i]) for i, (a, v, o) in enumerate(arrays)]
+    cut = [pl.ds(i * (SHARD // 4), SHARD // 4) for i in range(4)]
+    trips = [(u.at[0, at], uv.at[0, at], u_out.at[0, at]) for at in cut]
+    trips += [(d.at[0, at], dv.at[0, at], d_out.at[0, at]) for at in cut]
+    trips += [(m, mv, m_out), (t, tv, t_out)]
+    loads = [pltpu.make_async_copy(a, v, sem.at[i]) for i, (a, v, o) in enumerate(trips)]
     for copy in loads:
         copy.start()
     g_out[...] = g[:, :TOKS]
     stores = []
-    for i, (a, v, o) in enumerate(arrays):
+    for i, (a, v, o) in enumerate(trips):
         loads[i].wait()
         stores.append(pltpu.make_async_copy(v, o, sem_out.at[i]))
         stores[i].start()
@@ -500,7 +529,7 @@
             jax.ShapeDtypeStruct((1, SHARD, FFW), BF16),
         ),
         in_specs=[hbm, hbm, vmem, vmem, hbm, hbm],
-        out_specs=[vmem] * 5,
+        out_specs=[hbm, hbm, vmem, hbm, hbm],
         scratch_shapes=[
             pltpu.VMEM((NZ, TOKS, D), BF16),
             pltpu.VMEM((NZ, TOKS, D), BF16),
@@ -522,8 +551,8 @@
             pltpu.VMEM((NZ, TOKS, D), F32),
             pltpu.VMEM((NZ, TOP, LANES), F32),
             pltpu.VMEM((HALF + 1, TOKS, D), BF16),
-            pltpu.VMEM((HALF, TOKS, D), BF16),
-            pltpu.VMEM((HALF, TOKS, D), BF16),
+            pltpu.VMEM((HALF + 1, TOKS, D), BF16),
+            pltpu.VMEM((HALF + 1, TOKS, D), BF16),
             pltpu.VMEM((HALF + 1, TOKS, D), BF16),
             pltpu.VMEM((HALF + 1, TOP, LANES), F32),
             pltpu.VMEM((HALF, TOP, LANES), F32),
@@ -533,6 +562,8 @@
             pltpu.VMEM((2, SHARD // 2, FFW), BF16),
             pltpu.VMEM((2, SHARD, 2 * FFW), BF16),
             pltpu.VMEM((2, SHARD, FFW), BF16),
+            pltpu.VMEM((TOKS, D), BF16),
+            pltpu.VMEM((TOKS, D), BF16),
             pltpu.SemaphoreType.DMA((N_SEM,)),
             pltpu.SemaphoreType.DMA((N_SEM,)),
             pltpu.SemaphoreType.DMA((4 + 4 * BATCHES,)),
@@ -559,8 +590,8 @@
             pltpu.VMEM((TOKS, D), BF16),
             pltpu.VMEM((1, SHARD, 2 * FFW), BF16),
             pltpu.VMEM((1, SHARD, FFW), BF16),
-            pltpu.SemaphoreType.DMA((4,)),
-            pltpu.SemaphoreType.DMA((4,)),
+            pltpu.SemaphoreType.DMA((10,)),
+            pltpu.SemaphoreType.DMA((10,)),
         ],
         name="hand_over",
     )(*out)

time: 115 us -> 113 us (0.983)
    pallas_call x1, Pallas kernels: 111 us -> 109 us  [body(): pl.pallas_call(kernel, out_shape=(jax.ShapeDtypeStruct((TOKS, D), BF16),...]
where the time goes in v2:
time: 113 us
  Pallas kernels  113 us (100%)
    pallas_call x1, Pallas kernels, body(): pl.pallas_call(kernel, out_shape=(jax.ShapeDtypeStruct((TOKS, D), BF16),...  109 us
    pallas_call x1, Pallas kernels, body(): pl.pallas_call(hand_over, out_shape=(jax.ShapeDtypeStruct((TOKS, D), BF16...  3.53 us

profile of v2, /device:TPU:1, one launch (start us, length us, event | category | flops | bytes accessed | tf_op | source)
XLA Modules:
  0.0 113.2 jit_solution(17901357072112305989)
XLA Ops:
  0.6 109.0 %routed_layer.1 = (bf16[24,2048]{1,0:T(8,128)(2,1)}, bf16[24,2048]{1,0:T(8,128)(2,1)}, f32[8,128]{1,0:T(8,128)}, bf16[1,512,768]{2,1,0:T(8,128)(2,1)}, bf16[1,512,384]{2,1,0:T(8,128)(2,1)}) custom-call(bf16[24,2048]{1,0:T(8,128)(2,1)} %tok.1, bf16[24,2048]{1,0:T(8,128)(2,1)} %cot.1, s32[8,24]{1,0:T(8,128)} %bitcast.3, f32[8,24]{1,0:T(8,128)} %bitcast.4, ...), custom_call_target="tpu_custom_call" | custom-call | tf_op jit(solution)/shard_map/routed_layer/pallas_call | solution.py:522
  109.6 3.5 %hand_over.1 = (bf16[24,2048]{1,0:T(8,128)(2,1)}, bf16[24,2048]{1,0:T(8,128)(2,1)}, f32[8,24]{1,0:T(8,128)}, bf16[1,512,768]{2,1,0:T(8,128)(2,1)}, bf16[1,512,384]{2,1,0:T(8,128)(2,1)}) custom-call(bf16[24,2048]{1,0:T(8,128)(2,1)} %get-tuple-element.15.m, bf16[24,2048]{1,0:T(8,128)(2,1)} %get-tuple-element.16.t, f32[8,128]{1,0:T(8,128)} %get-tuple-element.17.g, ...), custom_call_target="tpu_custom_call" | custom-call | tf_op jit(solution)/shard_map/hand_over/pallas_call | solution.py:577

commit v3 on v2

--- a/solution.py
+++ b/solution.py
@@ -339,10 +339,14 @@
     far_right, far_left, near = [], [], []
 
     def far_grads():
-        weight_grads(2)
-        for gp, x2, x1 in grads:
-            far_right.append(send(gp.at[2, halves[0]], x2.at[0], "dp", right))
-            far_left.append(send(gp.at[2, halves[1]], x2.at[1], "dp", left))
+        slot = (x + 2) % NX
+        size = SHARD // 2
+        for start, right_side, (gp, x2, x1) in zip((0, NEXT), (pair, hs), grads):
+            for h, target, sent in ((0, right, far_right), (1, left, far_left)):
+                at = pl.ds(pl.multiple_of(start + slot * SHARD + h * size, LANES), size)
+                piece = rows[:, :, at].reshape(ROWS, size)
+                gp[2, halves[h], :] = dot(piece, right_side[...], (0, 0)).astype(BF16)
+                sent.append(send(gp.at[2, halves[h]], x2.at[h], "dp", target))
 
     def right_grads():
         weight_grads(1)
@@ -408,11 +412,11 @@
             flow("m", 1, k, um, pm, h)
 
     def token_step(k):
-        flow("g", -1, k, dg, ggp)
-        flow("g", 1, k, ug, ggp)
         for h in range(2):
             flow("t", -1, k, dd, pt, h)
             flow("t", 1, k, ud, pt, h)
+        flow("g", -1, k, dg, ggp)
+        flow("g", 1, k, ug, ggp)
 
     settled = []
 
@@ -432,10 +436,10 @@
         back = dot(pair[...], wgf[i], (1, 1)).astype(BF16)
         ob[:, :, NEXT + i * TILE : NEXT + (i + 1) * TILE] = back.reshape(ROWS // 8, 8, TILE)
     back_rows[3, 1] = send_back(3, 1)
+    combine(3, 0)
+    mixed_step(1)
     back_rows[2, 0] = send_back(2, 0)
     back_rows[2, 1] = send_back(2, 1)
-    combine(3, 0)
-    mixed_step(1)
     combine(3, 1)
     token_step(1)
     back_rows[1, 0] = send_back(1, 0)

time: 113 us -> 113 us (level)
  no operation moved by 1% of the time
where the time goes in v3:
time: 113 us
  Pallas kernels  112 us (99%)
    pallas_call x1, Pallas kernels, body(): pl.pallas_call(kernel, out_shape=(jax.ShapeDtypeStruct((TOKS, D), BF16),...  108 us
    pallas_call x1, Pallas kernels, body(): pl.pallas_call(hand_over, out_shape=(jax.ShapeDtypeStruct((TOKS, D), BF16...  3.53 us

profile of v3, /device:TPU:1, one launch (start us, length us, event | category | flops | bytes accessed | tf_op | source)
XLA Modules:
  0.0 112.5 jit_solution(14357864158774784898)
XLA Ops:
  0.6 108.4 %routed_layer.1 = (bf16[24,2048]{1,0:T(8,128)(2,1)}, bf16[24,2048]{1,0:T(8,128)(2,1)}, f32[8,128]{1,0:T(8,128)}, bf16[1,512,768]{2,1,0:T(8,128)(2,1)}, bf16[1,512,384]{2,1,0:T(8,128)(2,1)}) custom-call(bf16[24,2048]{1,0:T(8,128)(2,1)} %tok.1, bf16[24,2048]{1,0:T(8,128)(2,1)} %cot.1, s32[8,24]{1,0:T(8,128)} %bitcast.3, f32[8,24]{1,0:T(8,128)} %bitcast.4, ...), custom_call_target="tpu_custom_call" | custom-call | tf_op jit(solution)/shard_map/routed_layer/pallas_call | solution.py:526
  109.0 3.5 %hand_over.1 = (bf16[24,2048]{1,0:T(8,128)(2,1)}, bf16[24,2048]{1,0:T(8,128)(2,1)}, f32[8,24]{1,0:T(8,128)}, bf16[1,512,768]{2,1,0:T(8,128)(2,1)}, bf16[1,512,384]{2,1,0:T(8,128)(2,1)}) custom-call(bf16[24,2048]{1,0:T(8,128)(2,1)} %get-tuple-element.15.m, bf16[24,2048]{1,0:T(8,128)(2,1)} %get-tuple-element.16.t, f32[8,128]{1,0:T(8,128)} %get-tuple-element.17.g, ...), custom_call_target="tpu_custom_call" | custom-call | tf_op jit(solution)/shard_map/hand_over/pallas_call | solution.py:581
